TPU v7x, 256 devices: a whole 4x4x8 slice. The times are simulated.
256 devices in a mesh: dp: 8 (over z), vocab: 32 (over y, x, core).
Axes of the slice: x: 4, y: 4, z: 8, core: 2. Of those that a mesh axis runs over, the one named last changes fastest.
Arguments:
- teacher_hidden: bfloat16 [1024, 16384], P('vocab', 'dp'), may hold values from -40 to 40
- teacher_weight: bfloat16 [16384, 65536], P('dp', 'vocab'), may hold values from -0.140625 to 0.140625
- student_hidden: bfloat16 [1024, 4096], P('vocab', 'dp'), may hold values from -40 to 40
- student_weight: bfloat16 [4096, 65536], P('dp', 'vocab'), may hold values from -0.28125 to 0.28125
Outputs:
- token_kl: float32 [1024], P('dp')
- weight_grad: bfloat16 [4096, 65536], P('dp', 'vocab')
All inputs are finite; a program needn't handle non-finite values.
Results may differ from a plain program's by a relative error of at most 0.005.
Values may be sent and summed in bfloat16 or wider, within the bound.
A program may use at most 128 MiB of HBM per device.

v0:
```python
import jax
import jax.numpy as jnp
from jax import lax
from jax.sharding import PartitionSpec as P


def joined_along(parts, dim):
    lengths = list(parts.shape[1:])
    lengths[dim] *= parts.shape[0]
    return jnp.moveaxis(parts, 0, dim).reshape(lengths)


def copy_for_each(x, axis):
    copies = jnp.broadcast_to(x, (lax.axis_size(axis), *x.shape))
    return lax.all_to_all(copies, axis, split_axis=0, concat_axis=0, tiled=True)


def gather_directly(x, axis, dim):
    return joined_along(copy_for_each(x, axis), dim)


def collected_together(x, axis):
    leaves = jax.tree.leaves(x)
    order = sorted(range(len(leaves)), key=lambda k: -leaves[k].size)
    width = (1, *leaves[order[0]].shape)[-1]
    lines = [
        jnp.pad(leaves[k].reshape(-1), (0, -leaves[k].size % width)).reshape(-1, width)
        for k in order
    ]
    both, at, found = (copy_for_each(jnp.concatenate(lines), axis), 0, {})
    for k, line in zip(order, lines):
        piece = both[:, at : at + len(line)].reshape(len(both), -1)
        found[k] = piece[:, : leaves[k].size].reshape(-1, *leaves[k].shape)
        at += len(line)
    numbers = iter(range(len(leaves)))
    return jax.tree.map(lambda _: found[next(numbers)], x)


def joined_by_halves(pieces, combine):
    while len(jax.tree.leaves(pieces)[0]) > 1:
        pieces = jax.vmap(combine)(
            *(jax.tree.map(lambda part: part[side::2], pieces) for side in (0, 1))
        )
    return jax.tree.map(lambda part: part[0], pieces)


def joined_all(x, axis, combine):
    pieces = collected_together(x, axis)
    return joined_by_halves(pieces, combine)


def merge_stats(first, second):
    teacher_top = jnp.maximum(first[0], second[0])
    first_factor = jnp.exp(first[0] - teacher_top)
    second_factor = jnp.exp(second[0] - teacher_top)
    student_top = jnp.maximum(first[3], second[3])
    first_student = jnp.exp(first[3] - student_top)
    second_student = jnp.exp(second[3] - student_top)
    return (
        teacher_top,
        first[1] * first_factor + second[1] * second_factor,
        first[2] * first_factor + second[2] * second_factor,
        student_top,
        first[4] * first_student + second[4] * second_student,
    )


def body(teacher_hidden, teacher_weight, student_hidden, student_weight):
    vocab_count = lax.axis_size("vocab")
    student_rows = gather_directly(student_hidden, "vocab", 0)
    teacher_terms = jnp.dot(
        lax.all_gather(teacher_hidden, "vocab", axis=0, tiled=True),
        teacher_weight,
        preferred_element_type=jnp.float32,
    )
    width = teacher_terms.shape[1]
    teacher_logits = lax.psum_scatter(teacher_terms, "dp", scatter_dimension=0, tiled=True)
    block_rows = student_rows
    student_logits = lax.psum_scatter(
        jnp.dot(block_rows, student_weight, preferred_element_type=jnp.float32),
        "dp",
        scatter_dimension=0,
        tiled=True,
    )
    teacher_top = jnp.max(teacher_logits, axis=1)
    student_top = jnp.max(student_logits, axis=1)
    teacher_exp = jnp.exp(teacher_logits - teacher_top[:, None])
    local_stats = (
        teacher_top,
        jnp.sum(teacher_exp, axis=1),
        jnp.sum(teacher_exp * (teacher_logits - student_logits), axis=1),
        student_top,
        jnp.sum(jnp.exp(student_logits - student_top[:, None]), axis=1),
    )
    teacher_top, teacher_total, numerator, student_top, student_total = joined_all(
        local_stats, "vocab", merge_stats
    )
    teacher_lse = teacher_top + jnp.log(teacher_total)
    student_lse = student_top + jnp.log(student_total)
    token_kl = numerator / teacher_total - teacher_lse + student_lse
    vocab_total = width * vocab_count
    factor = vocab_total // 4 / student_rows.shape[0]
    teacher_prob = jnp.exp(teacher_logits - teacher_lse[:, None])
    student_prob = jnp.exp(student_logits - student_lse[:, None])
    deltas = (factor * (student_prob - teacher_prob)).astype(jnp.bfloat16)
    block_rows = student_rows
    product = lax.dot_general(
        block_rows,
        lax.all_gather(deltas, "dp", axis=0, tiled=True),
        (((0,), (0,)), ((), ())),
        preferred_element_type=jnp.float32,
    )
    return (token_kl, product.astype(jnp.bfloat16))


def solution(mesh):
    placed = (P("vocab", "dp"), P("dp", "vocab"), P("vocab", "dp"), P("dp", "vocab"))
    return jax.shard_map(
        body, mesh=mesh, in_specs=placed, out_specs=(P("dp"), P("dp", "vocab")), check_vma=False
    )
```

profile of v0, /device:TPU:1, one launch (start us, length us, event | category | flops | bytes accessed | tf_op | source)
XLA Modules:
  0.0 321.9 jit_solution(11014035527995620072)
XLA Ops:
  8.0 0.0 copy-start
  8.0 0.0 all-gather.3.cloned.1.call-start
  8.1 0.7 all-gather.3.cloned.1.call-update
  8.7 0.0 reduce-scatter.5.cloned.1.call-start
  8.8 0.9 broadcast_in_dim.4
  9.7 26.1 %all_to_all.10 = bf16[32,32,512]{2,1,0:T(8,128)(2,1)S(1)} all-to-all(bf16[32,32,512]{2,1,0:T(8,128)(2,1)S(1)} %broadcast_in_dim.4), channel_id=1, replica_groups=mesh['dp'=8,'vocab'=32] {'vocab'}, dimensions={0} | all-to-all | bytes 2097152 | tf_op jit(solution)/shard_map/all_to_all | solution.py:15
  35.8 0.0 copy-start.2
  35.8 1.0 copy-done.2
  36.8 0.0 copy-done
  36.8 5.6 %fusion.7 = f32[1024,2048]{1,0:T(8,128)} fusion(bf16[1024,512]{1,0:T(8,128)(2,1)S(1)} %bitcast.35, bf16[512,2048]{1,0:T(8,128)(2,1)S(1)} %copy-done), kind=kOutput, calls=%fused_computation.41 | convolution fusion | flops 2147483648 | bytes 11534336 | tf_op jit(solution)/shard_map/dot_general | solution.py:80
  42.3 0.0 reduce-scatter.5.cloned.1.call-update
  42.4 0.0 reduce-scatter.3.cloned.1.call-start
  42.4 26.8 %all-gather.3.cloned.1.call-done = bf16[1024,2048]{1,0:T(8,128)(2,1)} async-done(((bf16[32,2048]{1,0:T(8,128)(2,1)}), bf16[1024,2048]{1,0:T(8,128)(2,1)}) %all-gather.3.cloned.1.call-update) | async-done | bytes 4194320 | tf_op jit(solution)/shard_map/all_gather | solution.py:72
  69.2 14.6 %fusion.6 = f32[1024,2048]{1,0:T(8,128)} fusion(bf16[1024,2048]{1,0:T(8,128)(2,1)} %all-gather.3.cloned.1.call-done, bf16[2048,2048]{1,0:T(8,128)(2,1)} %param.5), kind=kOutput, calls=%fused_computation.40 | convolution fusion | flops 8589934592 | bytes 20971520 | tf_op jit(solution)/shard_map/dot_general | solution.py:71
  83.8 0.0 reduce-scatter.3.cloned.1.call-update
  83.8 0.0 all-gather.5.cloned.1.call-start
  83.8 52.5 %reduce-scatter.5.cloned.1.call-done = f32[128,2048]{1,0:T(8,128)} async-done(((f32[1024,2048]{1,0:T(8,128)}), f32[128,2048]{1,0:T(8,128)}) %reduce-scatter.5.cloned.1.call-update) | async-done | bytes 1048592 | tf_op jit(solution)/shard_map/reduce_scatter | solution.py:79
  136.3 0.0 copy-start.1
  136.3 1.4 reduce_max.19
  137.8 94.5 %reduce-scatter.3.cloned.1.call-done = f32[128,2048]{1,0:T(8,128)} async-done(((f32[1024,2048]{1,0:T(8,128)}), f32[128,2048]{1,0:T(8,128)}) %reduce-scatter.3.cloned.1.call-update) | async-done | bytes 1048592 | tf_op jit(solution)/shard_map/reduce_scatter | solution.py:77
  232.2 1.4 reduce_max.18
  233.6 2.1 multiply_reduce_fusion
  235.7 15.1 %all_to_all.11 = f32[32,5,128]{2,1,0:T(8,128)S(1)} all-to-all(f32[32,5,128]{2,1,0:T(8,128)S(1)} %broadcast_in_dim.5), channel_id=1, replica_groups=mesh['dp'=8,'vocab'=32] {'vocab'}, dimensions={0} | all-to-all | bytes 163840 | tf_op jit(solution)/shard_map/all_to_all | solution.py:15
  250.8 0.1 fusion.5
  251.7 0.5 fusion.2
  252.2 0.0 copy-done.1
  252.2 2.4 multiply_convert_fusion
  254.6 0.0 all-gather.5.cloned.1.call-update
  254.7 49.6 %all-gather.5.cloned.1.call-done = bf16[1024,2048]{1,0:T(8,128)(2,1)} async-done(((bf16[128,2048]{1,0:T(8,128)(2,1)}), bf16[1024,2048]{1,0:T(8,128)(2,1)}) %all-gather.5.cloned.1.call-update) | async-done | bytes 4194320 | tf_op jit(solution)/shard_map/all_gather | solution.py:109
  304.2 6.2 %fusion = bf16[512,2048]{0,1:T(8,128)(2,1)} fusion(bf16[1024,2048]{1,0:T(8,128)(2,1)} %all-gather.5.cloned.1.call-done, bf16[1024,512]{1,0:T(8,128)(2,1)} %bitcast.36), kind=kOutput, calls=%fused_computation.1 | convolution fusion | flops 2148532224 | bytes 7340032 | tf_op jit(solution)/shard_map/dot_general | solution.py:107
  310.4 3.9 %copy.10 = bf16[512,2048]{1,0:T(8,128)(2,1)} copy(bf16[512,2048]{0,1:T(8,128)(2,1)} %fusion) | data formatting | bytes 4194304
  (53 shorter events, 0.8 us)
Async XLA Ops:
  8.0 28.8 %copy-start = (bf16[512,2048]{1,0:T(8,128)(2,1)S(1)}, bf16[512,2048]{1,0:T(8,128)(2,1)}, u32[]{:S(2)}) copy-start(bf16[512,2048]{1,0:T(8,128)(2,1)} %param.7) | copy-start | bytes 6291460
  8.0 61.2 %all-gather.3.cloned.1.call-start = ((), (), s32[]{:S(2)}) async-start(), calls=%async_computation.4 | async-start | bytes 4325376 | tf_op jit(solution)/shard_map/all_gather | solution.py:72
  8.7 127.6 %reduce-scatter.5.cloned.1.call-start = ((), (), s32[]{:S(2)}) async-start(), calls=%async_computation.6 | async-start | bytes 9437184 | tf_op jit(solution)/shard_map/reduce_scatter | solution.py:79
  35.8 1.0 copy-start.2
  42.4 189.9 %reduce-scatter.3.cloned.1.call-start = ((), (), s32[]{:S(2)}) async-start(), calls=%async_computation.5 | async-start | bytes 9437184 | tf_op jit(solution)/shard_map/reduce_scatter | solution.py:77
  83.8 220.4 %all-gather.5.cloned.1.call-start = ((), (), s32[]{:S(2)}) async-start(), calls=%async_computation.7 | async-start | bytes 4718592 | tf_op jit(solution)/shard_map/all_gather | solution.py:109
  136.3 115.9 %copy-start.1 = (f32[128,2048]{1,0:T(8,128)S(1)}, f32[128,2048]{1,0:T(8,128)}, u32[]{:S(2)}) copy-start(f32[128,2048]{1,0:T(8,128)} %reduce-scatter.5.cloned.1.call-done) | copy-start | bytes 3145732
Sparse Core Ops, SparseCore 0:
  11.4 57.7 all-gather.2
Sparse Core Ops, SparseCore 1:
  42.4 93.8 reduce-scatter.4
  138.7 93.5 reduce-scatter.2
  254.8 49.4 all-gather.4
where the time goes:
time: 322 us
  waiting for transfers between devices  224 us (70%)
  blocking collectives  41.2 us (13%)
  matrix products  26.3 us (8%)
  between operations  15.8 us (5%)
  other arithmetic  7.95 us (2%)
  local copies, waits for them, and re-layouts  6.47 us (2%)
    reduce_scatter x1, waiting for transfers between devices, body(): lax.psum_scatter(teacher_terms, 'dp', scatter_dimension=0, tiled=True)  94.5 us
    reduce_scatter x1, waiting for transfers between devices, body(): lax.psum_scatter(jnp.dot(block_rows, student_weight, preferred_element_ty...  52.5 us
    all_gather x1, waiting for transfers between devices, body(): lax.all_gather(deltas, 'dp', axis=0, tiled=True)  49.6 us
    all_to_all x2, blocking collectives, copy_for_each(): return lax.all_to_all(copies, axis, split_axis=0, concat_axis=0, tiled=True)  41.2 us
    all_gather x1, waiting for transfers between devices, body(): lax.all_gather(teacher_hidden, 'vocab', axis=0, tiled=True)  26.8 us
    dot_general x1, matrix products, body(): jnp.dot(lax.all_gather(teacher_hidden, 'vocab', axis=0, tiled=True), teac...  14.6 us
  transfers between devices with their start and end apart: 4, of which 4 were waited for; matrix products, arithmetic and copies ran while one was open for 7% of the time, Pallas kernels for 0%

commit v1 on v0

v1 whole, which is shorter than its diff:
```python
import functools

import jax
import jax.numpy as jnp
from jax import lax
from jax.experimental import pallas as pl
from jax.experimental.pallas import tpu as pltpu
from jax.sharding import PartitionSpec as P

BF16 = jnp.bfloat16
F32 = jnp.float32
SCALE = 2.0**-7.75
LOG2E = 1.4426950408889634


def encode(x):
    t = jnp.abs(x) * SCALE + SCALE
    t = t * t
    t = t * t
    t = t * t
    t = t * t
    return jnp.where(x < 0, -t, t).astype(BF16)


def decode(word):
    y = word.astype(F32)
    t = jnp.exp2(jnp.log(jnp.abs(y)) * (LOG2E / 16) + 7.75) - 1.0
    return jnp.where(y < 0, -t, t)


def kernel(
    dims,
    th_hbm, tw_hbm, sh_hbm, sw_hbm,
    kl_out, grad_out,
    th, tw, sh, sw, pst, ptt, r_s, r_t, s_s, s_t, dl, acc, sht, stats,
    local_sem, hid_send, hid_recv, rel_send, rel_recv,
    s_send, s_recv, t_send, t_recv, st_send, st_recv, ag_send, ag_recv,
):
    nz, nv, cpq, gr, ks, kt, cq, tc, factor = dims
    nch = nv // 2
    n_items = 4 * (nz // 2 - 1) + 2
    p = lax.axis_index("dp")
    v = lax.axis_index("vocab")
    core = lax.rem(v, 2)
    chip = v // 2
    partner = v + 1 - 2 * core
    right, left = lax.rem(p + 1, nz), lax.rem(p + nz - 1, nz)
    ways = ((1, right), (-1, left))

    def at(offset):
        return lax.rem(p + offset + 2 * nz, nz)

    load_sw = pltpu.make_async_copy(sw_hbm, sw, local_sem.at[0])
    load_sh = pltpu.make_async_copy(sh_hbm, sh.at[core, chip], local_sem.at[1])
    load_th = pltpu.make_async_copy(th_hbm, th.at[core, chip], local_sem.at[2])
    load_sh.start()
    load_th.start()
    load_sw.start()
    n_tw = tw.shape[0]
    load_tw = [
        pltpu.make_async_copy(tw_hbm.at[:, j * tc : (j + 1) * tc], tw.at[j], local_sem.at[3 + j])
        for j in range(n_tw)
    ]
    for load in load_tw:
        load.start()

    barrier = pltpu.get_barrier_semaphore()

    def greet(j, _):
        pl.semaphore_signal(barrier, inc=1, device_id={"vocab": lax.rem(v + j, nv)})
        return 0

    lax.fori_loop(1, nv, greet, 0)
    for _, neighbour in ways:
        pl.semaphore_signal(barrier, inc=1, device_id={"dp": neighbour})
    pl.semaphore_wait(barrier, nv + 1)

    def spread(source, target, k):
        def one(j, _):
            peer = lax.rem(chip + j, nch)
            pltpu.make_async_remote_copy(
                source, target.at[core, chip], hid_send.at[k], hid_recv.at[k],
                device_id={"vocab": 2 * peer + core},
            ).start()
            return 0

        lax.fori_loop(1, nch, one, 0)

    def others(target, k):
        block = target.at[core, pl.ds(0, nch - 1)]
        return pltpu.make_async_remote_copy(
            block, block, hid_send.at[k], hid_recv.at[k], device_id={"vocab": partner}
        )

    def relay(target, k, slab):
        return pltpu.make_async_remote_copy(
            target.at[slab], target.at[slab], rel_send.at[k], rel_recv.at[k],
            device_id={"vocab": partner},
        )

    spread(sh_hbm, sh, 0)
    spread(th_hbm, th, 1)
    load_sh.wait()
    others(sh, 0).wait_recv()
    relay(sh, 0, core).start()
    load_sw.wait()
    relay(sh, 0, 1 - core).wait_recv()

    def student_block(q):
        rows = sh[:, pl.ds(cpq * q, cpq)].reshape(2 * gr, ks)
        for n in range(4):
            part = jnp.dot(rows, sw[:, n * cq : (n + 1) * cq], preferred_element_type=F32)
            pst[q, :, n] = part.reshape(2, gr, cq)

    def teacher_part(g, j):
        rows = th[g].reshape(nz * gr, kt)
        part = jnp.dot(rows, tw[j], preferred_element_type=F32)
        per = cq // tc
        cols = pl.ds(pl.multiple_of(lax.rem(j, per) * tc, tc), tc)
        ptt[:, g, j // per, :, cols] = part.reshape(nz, gr, tc)

    def student_copy(d, i, neighbour):
        return pltpu.make_async_remote_copy(
            s_s.at[d, i], r_s.at[d, i], s_send, s_recv.at[d, i], device_id={"dp": neighbour}
        )

    def teacher_copy(g, d, i, neighbour):
        return pltpu.make_async_remote_copy(
            s_t.at[g, d, i], r_t.at[g, d, i], t_send.at[g], t_recv.at[g, d, i],
            device_id={"dp": neighbour},
        )

    def student_items(lo, hi, more=None):
        def one(i, _):
            k = nz // 2 - (i + 2) // 4
            for d, (sign, neighbour) in enumerate(ways):
                n = lax.rem(i + 2 * d, 4)
                x = pst[at(sign * k), :, n]
                if lo >= 4:
                    student_copy(d, i - 4, neighbour).wait_recv()
                    x = x + decode(r_s[d, i - 4])
                s_s[d, i] = encode(x)
                student_copy(d, i, neighbour).start()
            if more is not None:
                more(i)
            return 0

        lax.fori_loop(lo, hi, one, 0)

    def student_end():
        def one(j, _):
            i = n_items - 4 + j
            for d, (_, neighbour) in enumerate(ways):
                n = lax.rem(i + 2 * d, 4)
                student_copy(d, i, neighbour).wait_recv()
                pst[p, :, n] = pst[p, :, n] + decode(r_s[d, i])
            return 0

        lax.fori_loop(0, 4, one, 0)

    def teacher_items(g, lo, hi, more=None):
        def one(i, _):
            k = nz // 2 - (i + 2) // 4
            for d, (sign, neighbour) in enumerate(ways):
                n = lax.rem(i + 2 * d, 4)
                x = ptt[at(sign * k), g, n]
                if lo >= 4:
                    teacher_copy(g, d, i - 4, neighbour).wait_recv()
                    x = x + decode(r_t[g, d, i - 4])
                s_t[g, d, i] = encode(x)
                teacher_copy(g, d, i, neighbour).start()
            if more is not None:
                more(i)
            return 0

        lax.fori_loop(lo, hi, one, 0)

    def teacher_end(g):
        def one(j, _):
            i = n_items - 4 + j
            for d, (_, neighbour) in enumerate(ways):
                n = lax.rem(i + 2 * d, 4)
                teacher_copy(g, d, i, neighbour).wait_recv()
                ptt[p, g, n] = ptt[p, g, n] + decode(r_t[g, d, i])
            return 0

        lax.fori_loop(0, 4, one, 0)

    def stats_start(g):
        t_top = jnp.full((gr, 1), -jnp.inf, F32)
        s_top = t_top
        for n in range(4):
            t_top = jnp.maximum(t_top, jnp.max(ptt[p, g, n], axis=1, keepdims=True))
            s_top = jnp.maximum(s_top, jnp.max(pst[p, g, n], axis=1, keepdims=True))
        t_sum = jnp.zeros((gr, 1), F32)
        t_num, s_sum = t_sum, t_sum
        for n in range(4):
            t, s = ptt[p, g, n], pst[p, g, n]
            e = jnp.exp(t - t_top)
            t_sum = t_sum + jnp.sum(e, axis=1, keepdims=True)
            t_num = t_num + jnp.sum(e * (t - s), axis=1, keepdims=True)
            s_sum = s_sum + jnp.sum(jnp.exp(s - s_top), axis=1, keepdims=True)
        lane = lax.broadcasted_iota(jnp.int32, (gr, 128), 1)
        table = jnp.zeros((gr, 128), F32)
        for place, column in ((0, t_top), (1, t_top), (2, s_top), (8, t_sum), (9, t_num), (10, s_sum)):
            table = jnp.where(lane == place, column, table)
        stats[g, v] = jnp.concatenate([table] * (128 // gr), axis=0).T[:16]

        def one(j, _):
            pltpu.make_async_remote_copy(
                stats.at[g, v], stats.at[g, v], st_send.at[g], st_recv.at[g],
                device_id={"vocab": lax.rem(v + j, nv)},
            ).start()
            return 0

        lax.fori_loop(1, nv, one, 0)

    def stats_copy(g):
        block = stats.at[g, pl.ds(0, nv - 1)]
        return pltpu.make_async_remote_copy(
            block, block, st_send.at[g], st_recv.at[g], device_id={"vocab": partner}
        )

    def deltas(g):
        stats_copy(g).wait_recv()
        tops = stats[g, :, 0:8]
        top = jnp.max(tops, axis=0)
        total = jnp.sum(jnp.exp(tops - top[None]) * stats[g, :, 8:16], axis=0)
        lse = top + jnp.log(total)
        kl_out[g : g + 1, :] = total[1:2] / total[0:1] - lse[0:1] + lse[2:3]
        turned = jnp.concatenate([lse] * 16, axis=0).T
        t_lse, s_lse = turned[:gr, 0:1], turned[:gr, 2:3]
        for n in range(4):
            student = jnp.exp(pst[p, g, n] - s_lse)
            teacher = jnp.exp(ptt[p, g, n] - t_lse)
            dl[g, n, p] = (factor * (student - teacher)).astype(BF16)

    def delta_copy(g, d, i, sign, neighbour):
        n = lax.rem(i + 2 * d, 4)
        block = dl.at[g, n, at(-sign * (i // 4))]
        return pltpu.make_async_remote_copy(
            block, block, ag_send.at[g], ag_recv.at[g, d, i], device_id={"dp": neighbour}
        )

    def arrived(g, d, i, sign, neighbour):
        n = lax.rem(i + 2 * d, 4)
        block = dl.at[g, n, at(-sign * (i // 4 + 1))]
        return pltpu.make_async_remote_copy(
            block, block, ag_send.at[g], ag_recv.at[g, d, i], device_id={"dp": neighbour}
        )

    def delta_items(g, lo, hi):
        def one(i, _):
            for d, (sign, neighbour) in enumerate(ways):
                if lo >= 4:
                    arrived(g, d, i - 4, sign, neighbour).wait_recv()
                delta_copy(g, d, i, sign, neighbour).start()
            return 0

        lax.fori_loop(lo, hi, one, 0)

    def delta_end(g):
        def one(i, _):
            for d, (sign, neighbour) in enumerate(ways):
                arrived(g, d, i, sign, neighbour).wait_recv()
            return 0

        lax.fori_loop(n_items - 4, n_items, one, 0)

    def grad_part(g, n):
        part = jnp.dot(sht[g], dl[g, n].reshape(nz * gr, cq), preferred_element_type=F32)
        if g == 0:
            acc[n] = part
        else:
            grad_out[:, n * cq : (n + 1) * cq] = (acc[n] + part).astype(BF16)

    last = n_items
    mid = max(4, last - 4)
    student_block(at(nz // 2))
    student_items(0, 2)
    for k in range(nz // 2 - 1, 0, -1):
        student_block(at(k))
        student_block(at(-k))
        if k == nz // 2 - 1:
            student_items(2, 4)
    student_block(p)
    for g in range(2):
        sht[g] = sh[g].reshape(nz * gr, ks).T
    student_items(4, mid)
    load_th.wait()
    others(th, 1).wait_recv()
    relay(th, 1, core).start()
    student_items(mid, last)
    for load in load_tw:
        load.wait()
    relay(th, 1, 1 - core).wait_recv()

    def teacher_first(j, _):
        teacher_part(0, j)
        return 0

    lax.fori_loop(0, n_tw, teacher_first, 0)
    teacher_items(0, 0, 4)
    student_end()

    def teacher_second(j, _):
        teacher_part(1, j)
        return 0

    lax.fori_loop(0, n_tw // 4, teacher_second, 0)
    teacher_items(0, 4, last)
    lax.fori_loop(n_tw // 4, n_tw, teacher_second, 0)
    teacher_items(1, 0, 4)
    teacher_end(0)
    stats_start(0)
    teacher_items(1, 4, mid)
    deltas(0)
    delta_items(0, 0, 4)
    teacher_items(1, mid, last)
    teacher_end(1)
    stats_start(1)
    delta_items(0, 4, mid)
    deltas(1)
    delta_items(1, 0, 4)
    delta_items(0, mid, last)
    delta_end(0)
    for n in range(4):
        grad_part(0, n)
    delta_items(1, 4, last)
    delta_end(1)
    for n in range(4):
        grad_part(1, n)

    others(sh, 0).wait_send()
    others(th, 1).wait_send()
    relay(sh, 0, core).wait_send()
    relay(th, 1, core).wait_send()
    pltpu.make_async_remote_copy(
        s_s, r_s, s_send, s_recv.at[0, 0], device_id={"dp": right}
    ).wait_send()
    for g in range(2):
        stats_copy(g).wait_send()
        for sem in (t_send, ag_send):
            pltpu.make_async_remote_copy(
                s_t.at[g], r_t.at[g], sem.at[g], t_recv.at[g, 0, 0], device_id={"dp": right}
            ).wait_send()


def body(teacher_hidden, teacher_weight, student_hidden, student_weight):
    nz, nv = lax.axis_size("dp"), lax.axis_size("vocab")
    rows, kt = teacher_hidden.shape
    ks, width = student_weight.shape
    nch = nv // 2
    cpq = nch // nz
    gr = cpq * rows
    cq = width // 4
    tc = min(256, cq)
    n_items = 4 * (nz // 2 - 1) + 2
    factor = float(width * nv // 4 / (rows * nv))
    dims = (nz, nv, cpq, gr, ks, kt, cq, tc, factor)
    dma = pltpu.SemaphoreType.DMA
    any_space = pl.BlockSpec(memory_space=pl.ANY)
    vmem = pl.BlockSpec(memory_space=pltpu.VMEM)
    kl, grad = pl.pallas_call(
        functools.partial(kernel, dims),
        out_shape=(
            jax.ShapeDtypeStruct((2, 128), F32),
            jax.ShapeDtypeStruct((ks, width), BF16),
        ),
        in_specs=[any_space] * 4,
        out_specs=(vmem, vmem),
        scratch_shapes=[
            pltpu.VMEM((2, nch, rows, kt), BF16),
            pltpu.VMEM((width // tc, kt, tc), BF16),
            pltpu.VMEM((2, nch, rows, ks), BF16),
            pltpu.VMEM((ks, width), BF16),
            pltpu.VMEM((nz, 2, 4, gr, cq), F32),
            pltpu.VMEM((nz, 2, 4, gr, cq), F32),
            pltpu.VMEM((2, n_items, 2, gr, cq), BF16),
            pltpu.VMEM((2, 2, n_items, gr, cq), BF16),
            pltpu.VMEM((2, n_items, 2, gr, cq), BF16),
            pltpu.VMEM((2, 2, n_items, gr, cq), BF16),
            pltpu.VMEM((2, 4, nz, gr, cq), BF16),
            pltpu.VMEM((4, ks, cq), F32),
            pltpu.VMEM((2, ks, nz * gr), BF16),
            pltpu.VMEM((2, nv, 16, 128), F32),
            dma((3 + width // tc,)),
            dma((2,)),
            dma((2,)),
            dma((2,)),
            dma((2,)),
            dma,
            dma((2, n_items)),
            dma((2,)),
            dma((2, 2, n_items)),
            dma((2,)),
            dma((2,)),
            dma((2,)),
            dma((2, 2, n_items)),
        ],
        compiler_params=pltpu.CompilerParams(
            collective_id=0, has_side_effects=True, vmem_limit_bytes=67_000_000
        ),
        name="distill",
    )(teacher_hidden, teacher_weight, student_hidden, student_weight)
    token_kl = kl[:, :gr].reshape(2, cpq, rows).transpose(1, 0, 2).reshape(2 * gr)
    return token_kl, grad


def solution(mesh):
    placed = (P("vocab", "dp"), P("dp", "vocab"), P("vocab", "dp"), P("dp", "vocab"))
    return jax.shard_map(
        body, mesh=mesh, in_specs=placed, out_specs=(P("dp"), P("dp", "vocab")), check_vma=False
    )
```

time: 322 us -> 170 us (0.53)
  waiting for transfers between devices: 224 us -> 0 us
  Pallas kernels: 0 us -> 163 us
  blocking collectives: 41.2 us -> 0 us
  matrix products: 26.3 us -> 0 us
  between operations: 15.8 us -> 0.64 us
  other arithmetic: 7.95 us -> 0 us
    pallas_call x0 -> x1, Pallas kernels: none -> 163 us  [body(): pl.pallas_call(functools.partial(kernel, dims), out_shape=(jax.ShapeDtype...]
    reduce_scatter x2 -> x0, waiting for transfers between devices: 147 us -> none  [the longest x1 94.5 us: body(): lax.psum_scatter(teacher_terms, 'dp', scatter_dimension=0, tiled=True)]
    all_gather x2 -> x0, waiting for transfers between devices: 76.3 us -> none  [the longest x1 49.6 us: body(): lax.all_gather(deltas, 'dp', axis=0, tiled=True)]
    all_to_all x2 -> x0, blocking collectives: 41.2 us -> none  [copy_for_each(): return lax.all_to_all(copies, axis, split_axis=0, concat_axis=0, tiled=True)]
    dot_general x3 -> x0, matrix products: 26.3 us -> none  [the longest x1 14.6 us: body(): jnp.dot(lax.all_gather(teacher_hidden, 'vocab', axis=0, tiled=True), teac...]
  transfers between devices with their start and end apart: 4 -> 0, of which waited for: 4 -> 0; matrix products, arithmetic and copies ran while one was open for 7% -> 0% of each run, Pallas kernels for 0% -> 0%
where the time goes in v1:
time: 170 us; the launch traced here: 168 us
  Pallas kernels  163 us (96%)
  local copies, waits for them, and re-layouts  4.51 us (3%)
    pallas_call x1, Pallas kernels, body(): pl.pallas_call(functools.partial(kernel, dims), out_shape=(jax.ShapeDtype...  163 us

profile of v1, /device:TPU:1, one launch (start us, length us, event | category | flops | bytes accessed | tf_op | source)
XLA Modules:
  0.0 168.1 jit_solution(3770532639030231966)
XLA Ops:
  0.6 162.9 %distill.1 = (f32[2,128]{1,0:T(2,128)}, bf16[512,2048]{1,0:T(8,128)(2,1)}) custom-call(bf16[32,2048]{1,0:T(8,128)(2,1)} %th_hbm.1, bf16[2048,2048]{1,0:T(8,128)(2,1)} %tw_hbm.1, bf16[32,512]{1,0:T(8,128)(2,1)} %sh_hbm.1, bf16[512,2048]{1,0:T(8,128)(2,1)} %sw_hbm.1), custom_call_target="tpu_custom_call" | custom-call | tf_op jit(solution)/shard_map/distill/pallas_call | solution.py:364
  163.6 0.7 reshape.10
  164.3 0.6 reshape.11
  164.9 3.2 %copy.8 = bf16[512,2048]{1,0:T(8,128)(2,1)} copy(bf16[512,2048]{1,0:T(8,128)(2,1)} %get-tuple-element.9) | data formatting | bytes 4194304
  (1 shorter events, 0.0 us)

commit v2 on v1

v2 whole, which is shorter than its diff:
```python
import functools

import jax
import jax.numpy as jnp
from jax import lax
from jax.experimental import pallas as pl
from jax.experimental.pallas import tpu as pltpu
from jax.sharding import PartitionSpec as P

BF16 = jnp.bfloat16
F32 = jnp.float32
SCALE = 2.0**-7.75
LOG2E = 1.4426950408889634


def encode(x):
    t = jnp.abs(x) * SCALE + SCALE
    t = t * t
    t = t * t
    t = t * t
    t = t * t
    return jnp.where(x < 0, -t, t).astype(BF16)


def decode(word):
    y = word.astype(F32)
    t = jnp.exp2(jnp.log(jnp.abs(y)) * (LOG2E / 16) + 7.75) - 1.0
    return jnp.where(y < 0, -t, t)


def kernel(
    dims,
    th_hbm, tw_hbm, sh_hbm, sw_hbm,
    kl_out, grad_out,
    th, tw, sh, sw, pst, ptt, r_s, r_t, s_s, s_t, dl, acc, sht, stats, stage,
    local_sem, hid_send, hid_recv, rel_send, rel_recv, out_sem,
    s_send, s_recv, t_send, t_recv, st_send, st_recv, ag_send, ag_recv,
):
    nz, nv, cpq, gr, ks, kt, cq, tc, factor = dims
    nch = nv // 2
    n_items = 4 * (nz // 2 - 1) + 2
    p = lax.axis_index("dp")
    v = lax.axis_index("vocab")
    core = lax.rem(v, 2)
    chip = v // 2
    partner = v + 1 - 2 * core
    right, left = lax.rem(p + 1, nz), lax.rem(p + nz - 1, nz)
    ways = ((1, right), (-1, left))

    def at(offset):
        return lax.rem(p + offset + 2 * nz, nz)

    load_sw = pltpu.make_async_copy(sw_hbm, sw, local_sem.at[0])
    load_sh = pltpu.make_async_copy(sh_hbm, sh.at[core, chip], local_sem.at[1])
    load_th = pltpu.make_async_copy(th_hbm, th.at[core, chip], local_sem.at[2])
    load_sh.start()
    load_th.start()
    load_sw.start()
    n_tw = tw.shape[0]
    load_tw = [
        pltpu.make_async_copy(tw_hbm.at[:, j * tc : (j + 1) * tc], tw.at[j], local_sem.at[3 + j])
        for j in range(n_tw)
    ]
    for load in load_tw:
        load.start()

    barrier = pltpu.get_barrier_semaphore()

    def greet(j, _):
        pl.semaphore_signal(barrier, inc=1, device_id={"vocab": lax.rem(v + j, nv)})
        return 0

    lax.fori_loop(1, nv, greet, 0)
    for _, neighbour in ways:
        pl.semaphore_signal(barrier, inc=1, device_id={"dp": neighbour})
    pl.semaphore_wait(barrier, nv + 1)

    def spread(source, target, k, arrival):
        def one(j, _):
            peer = lax.rem(chip + j, nch)
            pltpu.make_async_remote_copy(
                source, target.at[core, chip], hid_send.at[k], arrival,
                device_id={"vocab": 2 * peer + core},
            ).start()
            return 0

        lax.fori_loop(1, nch, one, 0)

    def others(target, k, arrival):
        block = target.at[core, pl.ds(0, nch - 1)]
        return pltpu.make_async_remote_copy(
            block, block, hid_send.at[k], arrival, device_id={"vocab": partner}
        )

    def relay(target, k, slab):
        return pltpu.make_async_remote_copy(
            target.at[slab], target.at[slab], rel_send.at[k], rel_recv.at[k],
            device_id={"vocab": partner},
        )

    spread(sh_hbm, sh, 0, hid_recv.at[chip])
    spread(th_hbm, th, 1, hid_recv.at[nch])
    load_sh.wait()
    load_sw.wait()

    def student_block(q):
        for j in range(cpq):
            source = cpq * q + j

            @pl.when(source != chip)
            def _():
                block = sh.at[core, source]
                pltpu.make_async_remote_copy(
                    block, block, hid_send.at[0], hid_recv.at[source], device_id={"vocab": partner}
                ).wait_recv()

        rows = sh[core, pl.ds(cpq * q, cpq)].reshape(gr, ks)
        for n in range(4):
            part = jnp.dot(rows, sw[:, n * cq : (n + 1) * cq], preferred_element_type=F32)
            pst[q, core, n] = part

    def student_rest():
        rows = sh[1 - core].reshape(nz * gr, ks)
        for n in range(4):
            part = jnp.dot(rows, sw[:, n * cq : (n + 1) * cq], preferred_element_type=F32)
            pst[:, 1 - core, n] = part.reshape(nz, gr, cq)

    def teacher_part(g, j):
        rows = th[g].reshape(nz * gr, kt)
        part = jnp.dot(rows, tw[j], preferred_element_type=F32)
        per = cq // tc
        cols = pl.ds(pl.multiple_of(lax.rem(j, per) * tc, tc), tc)
        ptt[:, g, j // per, :, cols] = part.reshape(nz, gr, tc)

    student = (pst, s_s, r_s, s_send, s_recv)
    teacher = (ptt, s_t, r_t, t_send, t_recv)

    def ring_copy(which, g, d, i, neighbour):
        _, out, landed, sent, got = which
        return pltpu.make_async_remote_copy(
            out.at[g, d, i], landed.at[g, d, i], sent.at[g], got.at[g, d, i],
            device_id={"dp": neighbour},
        )

    def ring_items(which, g, lo, hi, more=None):
        part, out, landed, _, _ = which

        def one(i, _):
            k = nz // 2 - (i + 2) // 4
            for d, (sign, neighbour) in enumerate(ways):
                n = lax.rem(i + 2 * d, 4)
                x = part[at(sign * k), g, n]
                if lo >= 4:
                    ring_copy(which, g, d, i - 4, neighbour).wait_recv()
                    x = x + decode(landed[g, d, i - 4])
                out[g, d, i] = encode(x)
                ring_copy(which, g, d, i, neighbour).start()
            if more is not None:
                more(i)
            return 0

        lax.fori_loop(lo, hi, one, 0)

    def ring_end(which, g):
        part, _, landed, _, _ = which

        def one(j, _):
            i = n_items - 4 + j
            for d, (_, neighbour) in enumerate(ways):
                n = lax.rem(i + 2 * d, 4)
                ring_copy(which, g, d, i, neighbour).wait_recv()
                part[p, g, n] = part[p, g, n] + decode(landed[g, d, i])
            return 0

        lax.fori_loop(0, 4, one, 0)

    def stats_start(g):
        t_top = jnp.full((gr, 1), -jnp.inf, F32)
        s_top = t_top
        for n in range(4):
            t_top = jnp.maximum(t_top, jnp.max(ptt[p, g, n], axis=1, keepdims=True))
            s_top = jnp.maximum(s_top, jnp.max(pst[p, g, n], axis=1, keepdims=True))
        t_sum = jnp.zeros((gr, 1), F32)
        t_num, s_sum = t_sum, t_sum
        for n in range(4):
            t, s = ptt[p, g, n], pst[p, g, n]
            e = jnp.exp(t - t_top)
            t_sum = t_sum + jnp.sum(e, axis=1, keepdims=True)
            t_num = t_num + jnp.sum(e * (t - s), axis=1, keepdims=True)
            s_sum = s_sum + jnp.sum(jnp.exp(s - s_top), axis=1, keepdims=True)
        lane = lax.broadcasted_iota(jnp.int32, (gr, 128), 1)
        table = jnp.zeros((gr, 128), F32)
        for place, column in ((0, t_top), (1, t_top), (2, s_top), (8, t_sum), (9, t_num), (10, s_sum)):
            table = jnp.where(lane == place, column, table)
        sides = [table[r : r + gr // cpq] for r in range(0, gr, gr // cpq) for _ in range(2)]
        stats[g, v] = jnp.concatenate(sides * (64 // gr), axis=0).T[:16]

        def one(j, _):
            pltpu.make_async_remote_copy(
                stats.at[g, v], stats.at[g, v], st_send.at[g], st_recv.at[g],
                device_id={"vocab": lax.rem(v + j, nv)},
            ).start()
            return 0

        lax.fori_loop(1, nv, one, 0)

    def stats_copy(g):
        block = stats.at[g, pl.ds(0, nv - 1)]
        return pltpu.make_async_remote_copy(
            block, block, st_send.at[g], st_recv.at[g], device_id={"vocab": partner}
        )

    def deltas(g):
        stats_copy(g).wait_recv()
        tops = stats[g, :, 0:8]
        top = jnp.max(tops, axis=0)
        total = jnp.sum(jnp.exp(tops - top[None]) * stats[g, :, 8:16], axis=0)
        lse = top + jnp.log(total)
        kl = total[1:2] / total[0:1] - lse[0:1] + lse[2:3]
        if g == 0:
            kl_out[...] = kl
        else:
            lane = lax.broadcasted_iota(jnp.int32, (1, 128), 1)
            kl_out[...] = jnp.where(lane // (gr // cpq) % 2 == 1, kl, kl_out[...])
        turned = jnp.concatenate([lse] * 16, axis=0).T
        rows = gr // cpq
        turned = jnp.concatenate([turned[2 * r : 2 * r + rows] for r in range(0, gr, rows)], axis=0)
        t_lse, s_lse = turned[:, 0:1], turned[:, 2:3]
        for n in range(4):
            by_student = jnp.exp(pst[p, g, n] - s_lse)
            by_teacher = jnp.exp(ptt[p, g, n] - t_lse)
            dl[g, n, p] = (factor * (by_student - by_teacher)).astype(BF16)

    def delta_copy(g, d, i, sign, neighbour):
        n = lax.rem(i + 2 * d, 4)
        block = dl.at[g, n, at(-sign * (i // 4))]
        return pltpu.make_async_remote_copy(
            block, block, ag_send.at[g], ag_recv.at[g, d, i], device_id={"dp": neighbour}
        )

    def arrived(g, d, i, sign, neighbour):
        n = lax.rem(i + 2 * d, 4)
        block = dl.at[g, n, at(-sign * (i // 4 + 1))]
        return pltpu.make_async_remote_copy(
            block, block, ag_send.at[g], ag_recv.at[g, d, i], device_id={"dp": neighbour}
        )

    def delta_items(g, lo, hi):
        def one(i, _):
            for d, (sign, neighbour) in enumerate(ways):
                if lo >= 4:
                    arrived(g, d, i - 4, sign, neighbour).wait_recv()
                delta_copy(g, d, i, sign, neighbour).start()
            return 0

        lax.fori_loop(lo, hi, one, 0)

    def delta_end(g, lo, hi):
        def one(i, _):
            for d, (sign, neighbour) in enumerate(ways):
                arrived(g, d, i, sign, neighbour).wait_recv()
            return 0

        lax.fori_loop(lo, hi, one, 0)

    def grad_copy(n):
        return pltpu.make_async_copy(
            stage.at[n], grad_out.at[:, n * cq : (n + 1) * cq], out_sem.at[n]
        )

    def grad_part(g, n):
        part = jnp.dot(sht[g], dl[g, n].reshape(nz * gr, cq), preferred_element_type=F32)
        if g == 0:
            acc[n] = part
        else:
            stage[n] = (acc[n] + part).astype(BF16)
            grad_copy(n).start()

    last = n_items
    mid = max(4, last - 4)
    other = 1 - core
    student_block(at(nz // 2))
    ring_items(student, core, 0, 2)
    for k in range(nz // 2 - 1, 0, -1):
        student_block(at(k))
        student_block(at(-k))
        if k == nz // 2 - 1:
            ring_items(student, core, 2, 4)
    student_block(p)
    relay(sh, 0, core).start()
    ring_items(student, core, 4, mid)
    relay(sh, 0, other).wait_recv()
    student_rest()
    ring_items(student, other, 0, 4)
    ring_items(student, core, mid, last)
    load_th.wait()
    others(th, 1, hid_recv.at[nch]).wait_recv()
    relay(th, 1, core).start()
    ring_end(student, core)
    for load in load_tw:
        load.wait()

    def teacher_own(i):
        @pl.when(i - 4 < n_tw)
        def _():
            teacher_part(core, i - 4)

    def teacher_rest(j, _):
        teacher_part(other, j)
        return 0

    ring_items(student, other, 4, last, teacher_own)
    for j in range(last - 4, n_tw):
        teacher_part(core, j)
    for g in range(2):
        sht[g] = sh[g].reshape(nz * gr, ks).T
    relay(th, 1, other).wait_recv()
    lax.fori_loop(0, n_tw, teacher_rest, 0)
    ring_items(teacher, 0, 0, 4)
    ring_end(student, other)
    ring_items(teacher, 0, 4, last)
    ring_items(teacher, 1, 0, 4)
    ring_end(teacher, 0)
    stats_start(0)
    ring_items(teacher, 1, 4, mid)
    deltas(0)
    delta_items(0, 0, 4)
    ring_items(teacher, 1, mid, last)
    ring_end(teacher, 1)
    stats_start(1)
    delta_items(0, 4, mid)
    deltas(1)
    delta_items(1, 0, 4)
    delta_items(0, mid, last)
    delta_items(1, 4, mid)
    delta_end(0, last - 4, last)
    for n in range(4):
        grad_part(0, n)
    delta_items(1, mid, last)
    delta_end(1, last - 4, last - 1)
    for n in (0, 2):
        grad_part(1, n)
    delta_end(1, last - 1, last)
    for n in (1, 3):
        grad_part(1, n)

    for n in range(4):
        grad_copy(n).wait()
    others(sh, 0, hid_recv.at[nch]).wait_send()
    others(th, 1, hid_recv.at[nch]).wait_send()
    relay(sh, 0, core).wait_send()
    relay(th, 1, core).wait_send()
    for g in range(2):
        stats_copy(g).wait_send()
        for sem in (s_send, t_send, ag_send):
            pltpu.make_async_remote_copy(
                s_t.at[g], r_t.at[g], sem.at[g], t_recv.at[g, 0, 0], device_id={"dp": right}
            ).wait_send()


def body(teacher_hidden, teacher_weight, student_hidden, student_weight):
    nz, nv = lax.axis_size("dp"), lax.axis_size("vocab")
    rows, kt = teacher_hidden.shape
    ks, width = student_weight.shape
    nch = nv // 2
    cpq = nch // nz
    gr = cpq * rows
    cq = width // 4
    tc = min(256, cq)
    n_items = 4 * (nz // 2 - 1) + 2
    factor = float(width * nv // 4 / (rows * nv))
    dims = (nz, nv, cpq, gr, ks, kt, cq, tc, factor)
    dma = pltpu.SemaphoreType.DMA
    any_space = pl.BlockSpec(memory_space=pl.ANY)
    vmem = pl.BlockSpec(memory_space=pltpu.VMEM)
    kl, grad = pl.pallas_call(
        functools.partial(kernel, dims),
        out_shape=(
            jax.ShapeDtypeStruct((1, 128), F32),
            jax.ShapeDtypeStruct((ks, width), BF16),
        ),
        in_specs=[any_space] * 4,
        out_specs=(vmem, any_space),
        scratch_shapes=[
            pltpu.VMEM((2, nch, rows, kt), BF16),
            pltpu.VMEM((width // tc, kt, tc), BF16),
            pltpu.VMEM((2, nch, rows, ks), BF16),
            pltpu.VMEM((ks, width), BF16),
            pltpu.VMEM((nz, 2, 4, gr, cq), F32),
            pltpu.VMEM((nz, 2, 4, gr, cq), F32),
            *[pltpu.VMEM((2, 2, n_items, gr, cq), BF16)] * 4,
            pltpu.VMEM((2, 4, nz, gr, cq), BF16),
            pltpu.VMEM((4, ks, cq), F32),
            pltpu.VMEM((2, ks, nz * gr), BF16),
            pltpu.VMEM((2, nv, 16, 128), F32),
            pltpu.VMEM((4, ks, cq), BF16),
            dma((3 + width // tc,)),
            dma((2,)),
            dma((nch + 1,)),
            dma((2,)),
            dma((2,)),
            dma((4,)),
            dma((2,)),
            dma((2, 2, n_items)),
            dma((2,)),
            dma((2, 2, n_items)),
            dma((2,)),
            dma((2,)),
            dma((2,)),
            dma((2, 2, n_items)),
        ],
        compiler_params=pltpu.CompilerParams(
            collective_id=0, has_side_effects=True, vmem_limit_bytes=67_000_000
        ),
        name="distill",
    )(teacher_hidden, teacher_weight, student_hidden, student_weight)
    return kl.reshape(128)[: 2 * gr], grad


def solution(mesh):
    placed = (P("vocab", "dp"), P("dp", "vocab"), P("vocab", "dp"), P("dp", "vocab"))
    return jax.shard_map(
        body, mesh=mesh, in_specs=placed, out_specs=(P("dp"), P("dp", "vocab")), check_vma=False
    )
```

time: 170 us -> 162 us (0.953)
  Pallas kernels: 163 us -> 157 us
    pallas_call x1, Pallas kernels: 163 us -> 157 us  [body(): pl.pallas_call(functools.partial(kernel, dims), out_shape=(jax.ShapeDtype...]
    unnamed x1 -> x2, local copies, waits for them, and re-layouts: 3.16 us -> 4.3 us
where the time goes in v2:
time: 162 us
  Pallas kernels  157 us (97%)
  local copies, waits for them, and re-layouts  4.3 us (3%)
    pallas_call x1, Pallas kernels, body(): pl.pallas_call(functools.partial(kernel, dims), out_shape=(jax.ShapeDtype...  157 us
    unnamed x2, local copies, waits for them, and re-layouts  4.3 us

profile of v2, /device:TPU:1, one launch (start us, length us, event | category | flops | bytes accessed | tf_op | source)
XLA Modules:
  0.0 161.6 jit_solution(8231750117445290847)
XLA Ops:
  0.6 156.7 %distill.1 = (f32[1,128]{1,0:T(1,128)}, bf16[512,2048]{1,0:T(8,128)(2,1)}) custom-call(bf16[32,2048]{1,0:T(8,128)(2,1)} %th_hbm.1, bf16[2048,2048]{1,0:T(8,128)(2,1)} %tw_hbm.1, bf16[32,512]{1,0:T(8,128)(2,1)} %sh_hbm.1, bf16[512,2048]{1,0:T(8,128)(2,1)} %sw_hbm.1), custom_call_target="tpu_custom_call" | custom-call | tf_op jit(solution)/shard_map/distill/pallas_call | solution.py:376
  157.3 1.1 copy.8
  158.4 3.2 %copy.9 = bf16[512,2048]{1,0:T(8,128)(2,1)} copy(bf16[512,2048]{1,0:T(8,128)(2,1)} %get-tuple-element.9) | data formatting | bytes 4194304

commit v3 on v2

--- a/solution.py
+++ b/solution.py
@@ -32,8 +32,8 @@
     dims,
     th_hbm, tw_hbm, sh_hbm, sw_hbm,
     kl_out, grad_out,
-    th, tw, sh, sw, pst, ptt, r_s, r_t, s_s, s_t, dl, acc, sht, stats, stage,
-    local_sem, hid_send, hid_recv, rel_send, rel_recv, out_sem,
+    th, tw, sh, sw, pst, ptt, r_s, r_t, s_s, s_t, dl, acc, sht, stats,
+    local_sem, hid_send, hid_recv, rel_send, rel_recv,
     s_send, s_recv, t_send, t_recv, st_send, st_recv, ag_send, ag_recv,
 ):
     nz, nv, cpq, gr, ks, kt, cq, tc, factor = dims
@@ -263,18 +263,12 @@
 
         lax.fori_loop(lo, hi, one, 0)
 
-    def grad_copy(n):
-        return pltpu.make_async_copy(
-            stage.at[n], grad_out.at[:, n * cq : (n + 1) * cq], out_sem.at[n]
-        )
-
     def grad_part(g, n):
         part = jnp.dot(sht[g], dl[g, n].reshape(nz * gr, cq), preferred_element_type=F32)
         if g == 0:
             acc[n] = part
         else:
-            stage[n] = (acc[n] + part).astype(BF16)
-            grad_copy(n).start()
+            grad_out[:, n * cq : (n + 1) * cq] = (acc[n] + part).astype(BF16)
 
     last = n_items
     mid = max(4, last - 4)
@@ -301,23 +295,31 @@
         load.wait()
 
     def teacher_own(i):
-        @pl.when(i - 4 < n_tw)
-        def _():
-            teacher_part(core, i - 4)
-
-    def teacher_rest(j, _):
-        teacher_part(other, j)
-        return 0
-
-    ring_items(student, other, 4, last, teacher_own)
-    for j in range(last - 4, n_tw):
-        teacher_part(core, j)
+        if n_items >= 14:
+            teacher_part(core, 2 * (i - 4))
+            teacher_part(core, 2 * (i - 4) + 1)
+
+    def teacher_rest(i):
+        if n_items >= 14:
+            teacher_part(other, i - 8)
+
+    def parts(slab, lo):
+        def one(j, _):
+            teacher_part(slab, j)
+            return 0
+
+        lax.fori_loop(lo, n_tw, one, 0)
+
+    early = min(8, last)
+    ring_items(student, other, 4, early, teacher_own)
+    parts(core, 8 if n_items >= 14 else 0)
+    relay(th, 1, other).wait_recv()
+    ring_items(student, other, early, last, teacher_rest)
+    parts(other, last - 8 if n_items >= 14 else 0)
+    ring_items(teacher, 0, 0, 4)
+    ring_end(student, other)
     for g in range(2):
         sht[g] = sh[g].reshape(nz * gr, ks).T
-    relay(th, 1, other).wait_recv()
-    lax.fori_loop(0, n_tw, teacher_rest, 0)
-    ring_items(teacher, 0, 0, 4)
-    ring_end(student, other)
     ring_items(teacher, 0, 4, last)
     ring_items(teacher, 1, 0, 4)
     ring_end(teacher, 0)
@@ -326,17 +328,19 @@
     deltas(0)
     delta_items(0, 0, 4)
     ring_items(teacher, 1, mid, last)
+    delta_items(0, 4, early)
     ring_end(teacher, 1)
     stats_start(1)
-    delta_items(0, 4, mid)
+    late = max(early, last - 2)
+    delta_items(0, early, late)
     deltas(1)
     delta_items(1, 0, 4)
-    delta_items(0, mid, last)
-    delta_items(1, 4, mid)
+    delta_items(0, late, last)
+    delta_items(1, 4, early)
     delta_end(0, last - 4, last)
     for n in range(4):
         grad_part(0, n)
-    delta_items(1, mid, last)
+    delta_items(1, early, last)
     delta_end(1, last - 4, last - 1)
     for n in (0, 2):
         grad_part(1, n)
@@ -344,8 +348,6 @@
     for n in (1, 3):
         grad_part(1, n)
 
-    for n in range(4):
-        grad_copy(n).wait()
     others(sh, 0, hid_recv.at[nch]).wait_send()
     others(th, 1, hid_recv.at[nch]).wait_send()
     relay(sh, 0, core).wait_send()
@@ -377,10 +379,10 @@
         functools.partial(kernel, dims),
         out_shape=(
             jax.ShapeDtypeStruct((1, 128), F32),
-            jax.ShapeDtypeStruct((ks, width), BF16),
+            pltpu.MemorySpace.VMEM((ks, width), BF16),
         ),
         in_specs=[any_space] * 4,
-        out_specs=(vmem, any_space),
+        out_specs=(vmem, vmem),
         scratch_shapes=[
             pltpu.VMEM((2, nch, rows, kt), BF16),
             pltpu.VMEM((width // tc, kt, tc), BF16),
@@ -393,13 +395,11 @@
             pltpu.VMEM((4, ks, cq), F32),
             pltpu.VMEM((2, ks, nz * gr), BF16),
             pltpu.VMEM((2, nv, 16, 128), F32),
-            pltpu.VMEM((4, ks, cq), BF16),
             dma((3 + width // tc,)),
             dma((2,)),
             dma((nch + 1,)),
             dma((2,)),
             dma((2,)),
-            dma((4,)),
             dma((2,)),
             dma((2, 2, n_items)),
             dma((2,)),
@@ -410,7 +410,7 @@
             dma((2, 2, n_items)),
         ],
         compiler_params=pltpu.CompilerParams(
-            collective_id=0, has_side_effects=True, vmem_limit_bytes=67_000_000
+            collective_id=0, has_side_effects=True, vmem_limit_bytes=64_500_000
         ),
         name="distill",
     )(teacher_hidden, teacher_weight, student_hidden, student_weight)

time: 162 us -> 156 us (0.963)
  Pallas kernels: 157 us -> 154 us
  local copies, waits for them, and re-layouts: 4.3 us -> 1.84 us
    pallas_call x1, Pallas kernels: 157 us -> 154 us  [body(): pl.pallas_call(functools.partial(kernel, dims), out_shape=(jax.ShapeDtype...]
    unnamed x2 -> x4, local copies, waits for them, and re-layouts: 4.3 us -> 1.84 us
where the time goes in v3:
time: 156 us
  Pallas kernels  154 us (99%)
  local copies, waits for them, and re-layouts  1.84 us (1%)
    pallas_call x1, Pallas kernels, body(): pl.pallas_call(functools.partial(kernel, dims), out_shape=(jax.ShapeDtype...  154 us

profile of v3, /device:TPU:1, one launch (start us, length us, event | category | flops | bytes accessed | tf_op | source)
XLA Modules:
  0.0 156.0 jit_solution(17060535980350619052)
XLA Ops:
  0.6 153.5 %distill.1 = (f32[1,128]{1,0:T(1,128)}, bf16[512,2048]{1,0:T(8,128)(2,1)S(1)}) custom-call(bf16[32,2048]{1,0:T(8,128)(2,1)} %th_hbm.1, bf16[2048,2048]{1,0:T(8,128)(2,1)} %tw_hbm.1, bf16[32,512]{1,0:T(8,128)(2,1)} %sh_hbm.1, bf16[512,2048]{1,0:T(8,128)(2,1)} %sw_hbm.1), custom_call_target="tpu_custom_call" | custom-call | tf_op jit(solution)/shard_map/distill/pallas_call | solution.py:378
  154.1 0.0 copy-start
  154.1 1.3 copy.8
  155.5 0.0 copy-done
  155.5 0.5 copy.9
Async XLA Ops:
  154.1 1.3 copy-start

commit v4 on v3

--- a/solution.py
+++ b/solution.py
@@ -287,47 +287,51 @@
     student_rest()
     ring_items(student, other, 0, 4)
     ring_items(student, core, mid, last)
+    ring_end(student, core)
+    ring_items(student, other, 4, mid)
     load_th.wait()
     others(th, 1, hid_recv.at[nch]).wait_recv()
     relay(th, 1, core).start()
-    ring_end(student, core)
+    late = max(mid, last - 2)
+    ring_items(student, other, mid, late)
     for load in load_tw:
         load.wait()
-
-    def teacher_own(i):
-        if n_items >= 14:
-            teacher_part(core, 2 * (i - 4))
-            teacher_part(core, 2 * (i - 4) + 1)
-
-    def teacher_rest(i):
-        if n_items >= 14:
-            teacher_part(other, i - 8)
-
-    def parts(slab, lo):
+    relay(th, 1, other).wait_recv()
+    full = n_tw == 8 and n_items == 14
+
+    def parts(g, lo):
         def one(j, _):
-            teacher_part(slab, j)
+            teacher_part(g, j)
             return 0
 
         lax.fori_loop(lo, n_tw, one, 0)
 
-    early = min(8, last)
-    ring_items(student, other, 4, early, teacher_own)
-    parts(core, 8 if n_items >= 14 else 0)
-    relay(th, 1, other).wait_recv()
-    ring_items(student, other, early, last, teacher_rest)
-    parts(other, last - 8 if n_items >= 14 else 0)
+    def first_parts(i):
+        if full:
+            teacher_part(0, 2 * (i - 12))
+            teacher_part(0, 2 * (i - 12) + 1)
+
+    def second_parts(i):
+        if full:
+            teacher_part(1, i - 4)
+
+    ring_items(student, other, late, last, first_parts)
+    parts(0, 4 if full else 0)
     ring_items(teacher, 0, 0, 4)
     ring_end(student, other)
-    for g in range(2):
-        sht[g] = sh[g].reshape(nz * gr, ks).T
-    ring_items(teacher, 0, 4, last)
+    ring_items(teacher, 0, 4, min(12, last), second_parts)
+    parts(1, 8 if full else 0)
+    ring_items(teacher, 0, max(4, min(12, last)), last)
     ring_items(teacher, 1, 0, 4)
     ring_end(teacher, 0)
     stats_start(0)
+    for g in range(2):
+        sht[g] = sh[g].reshape(nz * gr, ks).T
     ring_items(teacher, 1, 4, mid)
     deltas(0)
     delta_items(0, 0, 4)
     ring_items(teacher, 1, mid, last)
+    early = min(8, last)
     delta_items(0, 4, early)
     ring_end(teacher, 1)
     stats_start(1)

time: 156 us -> 157 us (level)
  no operation moved by 1% of the time
where the time goes in v4:
time: 157 us
  Pallas kernels  155 us (99%)
  local copies, waits for them, and re-layouts  1.84 us (1%)
    pallas_call x1, Pallas kernels, body(): pl.pallas_call(functools.partial(kernel, dims), out_shape=(jax.ShapeDtype...  155 us

profile of v4, /device:TPU:1, one launch (start us, length us, event | category | flops | bytes accessed | tf_op | source)
XLA Modules:
  0.0 157.1 jit_solution(6664454714665706817)
XLA Ops:
  0.6 154.7 %distill.1 = (f32[1,128]{1,0:T(1,128)}, bf16[512,2048]{1,0:T(8,128)(2,1)S(1)}) custom-call(bf16[32,2048]{1,0:T(8,128)(2,1)} %th_hbm.1, bf16[2048,2048]{1,0:T(8,128)(2,1)} %tw_hbm.1, bf16[32,512]{1,0:T(8,128)(2,1)} %sh_hbm.1, bf16[512,2048]{1,0:T(8,128)(2,1)} %sw_hbm.1), custom_call_target="tpu_custom_call" | custom-call | tf_op jit(solution)/shard_map/distill/pallas_call | solution.py:382
  155.3 0.0 copy-start
  155.3 1.3 copy.8
  156.6 0.0 copy-done
  156.6 0.5 copy.9
Async XLA Ops:
  155.3 1.3 copy-start

commit v5 on v3

--- a/solution.py
+++ b/solution.py
@@ -99,7 +99,65 @@
         )
 
     spread(sh_hbm, sh, 0, hid_recv.at[chip])
-    spread(th_hbm, th, 1, hid_recv.at[nch])
+    side = 4
+    turns = nch == side * side
+
+    def chip_at(dx, dy):
+        return lax.rem(chip // side + dy + side, side) * side + lax.rem(chip + dx + side, side)
+
+    def block_copy(source, block, to):
+        return pltpu.make_async_remote_copy(
+            source, th.at[core, block], hid_send.at[1], hid_recv.at[nch + block],
+            device_id={"vocab": 2 * to + core},
+        )
+
+    def teacher_direct():
+        spread(th_hbm, th, 1, hid_recv.at[nch + chip])
+
+    def teacher_near():
+        for dx, dy in ((3, 0), (0, 3), (3, 1), (1, 3), (3, 3), (1, 0), (0, 1), (1, 1)):
+            block_copy(th_hbm, chip, chip_at(dx, dy)).start()
+
+    if turns:
+        pl.when(core == 0)(teacher_direct)
+        pl.when(core == 1)(teacher_near)
+    else:
+        teacher_direct()
+
+    def teacher_from(block):
+        block_copy(th.at[core, block], block, lax.rem(chip + 1, nch)).wait_recv()
+
+    def teacher_forward(a, b, steps):
+        block = chip_at(-a, -b)
+        teacher_from(block)
+
+        @pl.when(core == 1)
+        def _():
+            for dx, dy in steps:
+                block_copy(th.at[core, block], block, chip_at(dx, dy)).start()
+
+    def forwards(group):
+        if turns:
+            for item in group:
+                teacher_forward(*item)
+
+    west, north = (-1, 0), (0, -1)
+    first_forwards = ((3, 0, (west,)), (0, 3, (north,)))
+    second_forwards = ((3, 1, (west,)), (1, 3, (north,)), (3, 3, (west, north)))
+    third_forwards = ((2, 3, (north,)),)
+
+    def teacher_others():
+        if turns:
+            for a, b in ((0, 1), (1, 0), (1, 1), (0, 2), (2, 0), (1, 2), (2, 1), (3, 2), (2, 2)):
+                teacher_from(chip_at(-a, -b))
+        else:
+
+            def one(j, _):
+                teacher_from(lax.rem(chip + j, nch))
+                return 0
+
+            lax.fori_loop(1, nch, one, 0)
+
     load_sh.wait()
     load_sw.wait()
 
@@ -283,12 +341,15 @@
     student_block(p)
     relay(sh, 0, core).start()
     ring_items(student, core, 4, mid)
+    forwards(first_forwards)
     relay(sh, 0, other).wait_recv()
     student_rest()
     ring_items(student, other, 0, 4)
+    forwards(second_forwards)
     ring_items(student, core, mid, last)
+    forwards(third_forwards)
     load_th.wait()
-    others(th, 1, hid_recv.at[nch]).wait_recv()
+    teacher_others()
     relay(th, 1, core).start()
     ring_end(student, core)
     for load in load_tw:
@@ -397,7 +458,7 @@
             pltpu.VMEM((2, nv, 16, 128), F32),
             dma((3 + width // tc,)),
             dma((2,)),
-            dma((nch + 1,)),
+            dma((2 * nch,)),
             dma((2,)),
             dma((2,)),
             dma((2,)),

time: 156 us -> 149 us (0.955)
  Pallas kernels: 154 us -> 147 us
    pallas_call x1, Pallas kernels: 154 us -> 147 us  [body(): pl.pallas_call(functools.partial(kernel, dims), out_shape=(jax.ShapeDtype...]
where the time goes in v5:
time: 149 us
  Pallas kernels  147 us (99%)
  local copies, waits for them, and re-layouts  1.84 us (1%)
    pallas_call x1, Pallas kernels, body(): pl.pallas_call(functools.partial(kernel, dims), out_shape=(jax.ShapeDtype...  147 us

profile of v5, /device:TPU:1, one launch (start us, length us, event | category | flops | bytes accessed | tf_op | source)
XLA Modules:
  0.0 149.1 jit_solution(16150125653079190564)
XLA Ops:
  0.6 146.6 %distill.1 = (f32[1,128]{1,0:T(1,128)}, bf16[512,2048]{1,0:T(8,128)(2,1)S(1)}) custom-call(bf16[32,2048]{1,0:T(8,128)(2,1)} %th_hbm.1, bf16[2048,2048]{1,0:T(8,128)(2,1)} %tw_hbm.1, bf16[32,512]{1,0:T(8,128)(2,1)} %sh_hbm.1, bf16[512,2048]{1,0:T(8,128)(2,1)} %sw_hbm.1), custom_call_target="tpu_custom_call" | custom-call | tf_op jit(solution)/shard_map/distill/pallas_call | solution.py:439
  147.3 0.0 copy-start
  147.3 1.3 copy.8
  148.6 0.0 copy-done
  148.6 0.5 copy.9
Async XLA Ops:
  147.3 1.3 copy-start
